TPU v7x, 128 devices: a whole 4x4x4 slice. The times are simulated.
128 devices in a mesh: pool: 16 (over x_lo, z, core), cp: 8 (over x_hi, y).
Axes of the slice: x: 4 (x_hi: 2, x_lo: 2; x = x_hi * 2 + x_lo), y: 4, z: 4, core: 2. Of those that a mesh axis runs over, the one named last changes fastest.
Arguments:
- queries: bfloat16 [16, 1024, 4096], P('pool', 'cp'), may hold values from -15 to 15
- span_keys: bfloat16 [16, 1024, 512], P('pool', 'cp'), may hold values from -6 to 6
- span_values: bfloat16 [16, 1024, 512], P('pool', 'cp'), may hold values from -6 to 6
- pool_keys: bfloat16 [384, 128, 512], P('pool'), may hold values from -6 to 6
- pool_values: bfloat16 [384, 128, 512], P('pool'), may hold values from -6 to 6
- page_ids: int32 [16, 32], replicated, may hold values from 0 to 383, as said below
- prefix_pages: int32 [16], replicated, may hold values from 1 to 32, as said below
Outputs:
- attended: float32 [16, 1024, 4096], P('pool', 'cp')
Inputs may be any that keep to these rules, and one draw needn't show every extreme that they name: `page_ids`: page p is held by index p // 24 of pool. Among the first prefix_pages[r] entries of a request, one owner holds at most 2 pages, all different; entries beyond that are unused. `prefix_pages`: some request has all 32 entries in use.
All inputs are finite; a program needn't handle non-finite values.
Results may differ from a plain program's by a relative error of at most 0.002.
Values may be sent and summed in bfloat16 or wider, within the bound.
A program may use at most 128 MiB of HBM per device.

v0:
```python
import jax
import jax.numpy as jnp
from jax import lax
from jax.sharding import PartitionSpec as P

HEAD_DIM = 128
HEADS = 32
KV_HEADS = 4
CAP = 2
PAGES_DEV = 24


NEG_FILL = -1e30


def attend(running, queries_grouped4, key_row_set, value_row_set, visible):
    total_rows = key_row_set.shape[0]
    block_len = 512
    blocks = total_rows // block_len
    score_scale = HEAD_DIM ** (-0.5)
    key_blocks = key_row_set.reshape(blocks, block_len, KV_HEADS, HEAD_DIM)
    value_blocks = value_row_set.reshape(blocks, block_len, KV_HEADS, HEAD_DIM)
    vis_blocks = visible.reshape(visible.shape[0], blocks, block_len).transpose(1, 0, 2)

    def block_step(carried, inputs):
        peak, denom, weighted_values = carried
        key_tile, value_tile, vis_block = inputs
        logit_scores = (
            jnp.einsum(
                "swxl,cwl->swxc", queries_grouped4, key_tile, preferred_element_type=jnp.float32
            )
            * score_scale
        )
        live = vis_block[:, None, None, :]
        logit_scores = jnp.where(live, logit_scores, NEG_FILL)
        new_peak = jnp.maximum(peak, jnp.max(logit_scores, axis=-1))
        softmax_weights = jnp.where(live, jnp.exp(logit_scores - new_peak[..., None]), 0.0).astype(
            jnp.bfloat16
        )
        factor = jnp.exp(peak - new_peak)
        denom = denom * factor + jnp.sum(softmax_weights, axis=-1, dtype=jnp.float32)
        weighted_values = weighted_values * factor[..., None] + jnp.einsum(
            "unqy,ynx->unqx", softmax_weights, value_tile, preferred_element_type=jnp.float32
        )
        return ((new_peak, denom, weighted_values), None)

    return lax.scan(block_step, running, (key_blocks, value_blocks, vis_blocks))[0]


def body(queries, span_keys, span_values, pool_keys, pool_values, page_ids, prefix_pages):
    tok_count = queries.shape[1]
    groups = HEADS // KV_HEADS
    width = KV_HEADS * HEAD_DIM
    queries_grouped4 = queries[0].reshape(tok_count, KV_HEADS, groups, HEAD_DIM)
    pool_count = lax.axis_size("pool")
    pool_index = lax.axis_index("pool")
    ctx_index = lax.axis_index("cp")
    slot_count = page_ids.shape[1]
    owners = page_ids // PAGES_DEV
    slot_iota = jnp.arange(slot_count, dtype=jnp.int32)
    live_slots = slot_iota[None, :] < prefix_pages[:, None]
    earlier = slot_iota[None, :] < slot_iota[:, None]
    same_owner = (owners[:, :, None] == owners[:, None, :]) & live_slots[:, None, :] & earlier[None]
    slot_rank = jnp.sum(same_owner.astype(jnp.int32), axis=2)
    held_here = live_slots & (owners == pool_index)
    cap_iota = jnp.arange(CAP, dtype=jnp.int32)
    picked = held_here[:, None, :] & (slot_rank[:, None, :] == cap_iota[None, :, None])
    local_pages = jnp.sum(jnp.where(picked, page_ids[:, None, :] % PAGES_DEV, 0), axis=2)
    own_owners = lax.dynamic_index_in_dim(owners, pool_index, 0, keepdims=False)
    own_live = lax.dynamic_index_in_dim(live_slots, pool_index, 0, keepdims=False)
    owner_iota = jnp.arange(pool_count, dtype=jnp.int32)
    per_owner = jnp.sum(
        ((own_owners[None, :] == owner_iota[:, None]) & own_live[None, :]).astype(jnp.int32), axis=1
    )
    usable = cap_iota[None, :] < per_owner[:, None]
    empty = (
        jnp.full((tok_count, KV_HEADS, groups), NEG_FILL, jnp.float32),
        jnp.zeros((tok_count, KV_HEADS, groups), jnp.float32),
        jnp.zeros((tok_count, KV_HEADS, groups, HEAD_DIM), jnp.float32),
    )
    query_pos = ctx_index * tok_count + jnp.arange(tok_count, dtype=jnp.int32)
    key_piece = lax.all_gather(span_keys, "cp", axis=1, tiled=True)
    value_piece = lax.all_gather(span_values, "cp", axis=1, tiled=True)
    piece_len = key_piece.shape[1]
    key_pos = jnp.arange(piece_len, dtype=jnp.int32)
    visible = key_pos[None, :] <= query_pos[:, None]
    local_state = attend(empty, queries_grouped4, key_piece[0], value_piece[0], visible)
    fetched_keys, fetched_values = (
        lax.all_to_all(pool_keys[local_pages], "pool", split_axis=0, concat_axis=0, tiled=True),
        lax.all_to_all(pool_values[local_pages], "pool", split_axis=0, concat_axis=0, tiled=True),
    )
    part_len = fetched_keys.shape[2]
    visible = jnp.broadcast_to(usable[:, :, None], (pool_count, CAP, part_len)).reshape(1, -1)
    prefix_state = attend(
        empty,
        queries_grouped4,
        fetched_keys.reshape(-1, width),
        fetched_values.reshape(-1, width),
        visible,
    )
    peak_one, denom_one, mixed_one = local_state
    peak_two, denom_two, mixed_two = prefix_state
    peak = jnp.maximum(peak_one, peak_two)
    factor_one = jnp.exp(peak_one - peak)
    factor_two = jnp.exp(peak_two - peak)
    denom = denom_one * factor_one + denom_two * factor_two
    weighted_values = mixed_one * factor_one[..., None] + mixed_two * factor_two[..., None]
    attended = weighted_values / denom[..., None]
    return attended.reshape(1, tok_count, HEADS * HEAD_DIM)


def solution(mesh):
    in_specs = (
        P("pool", "cp", None),
        P("pool", "cp", None),
        P("pool", "cp", None),
        P("pool", None, None),
        P("pool", None, None),
        P(),
        P(),
    )
    out_specs = P("pool", "cp", None)
    return jax.shard_map(body, mesh=mesh, in_specs=in_specs, out_specs=out_specs, check_vma=False)
```

profile of v0, /device:TPU:103, one launch (start us, length us, event | category | flops | bytes accessed | tf_op | source)
XLA Modules:
  0.0 374.7 jit_solution(9860635105908914886)
XLA Ops:
  11.8 6.0 %all-to-all-start = ((bf16[16,2,128,512]{3,2,1,0:T(8,128)(2,1)}), bf16[16,2,128,512]{3,2,1,0:T(8,128)(2,1)}, u32[]{:S(2)}, u32[]{:S(2)}) async-start(bf16[16,2,128,512]{3,2,1,0:T(8,128)(2,1)} %bitcast.101), calls=%async_computation | async-start | bytes 8388608 | tf_op jit(solution)/shard_map/all_to_all | solution.py:89
  25.0 46.9 %all-gather.5.cloned.1.call-done = bf16[1,1024,512]{2,1,0:T(8,128)(2,1)} async-done(((bf16[1,128,512]{2,1,0:T(8,128)(2,1)}), bf16[1,1024,512]{2,1,0:T(8,128)(2,1)}) %all-gather.5.cloned.1.call-update) | async-done | bytes 1048592 | tf_op jit(solution)/shard_map/all_gather | solution.py:83
  74.0 44.0 %all-gather.3.cloned.1.call-done = bf16[1,1024,512]{2,1,0:T(8,128)(2,1)} async-done(((bf16[1,128,512]{2,1,0:T(8,128)(2,1)}), bf16[1,1024,512]{2,1,0:T(8,128)(2,1)}) %all-gather.3.cloned.1.call-update) | async-done | bytes 1048592 | tf_op jit(solution)/shard_map/all_gather | solution.py:82
  120.2 7.5 %all-to-all-start.1 = ((bf16[16,2,128,512]{3,2,1,0:T(8,128)(2,1)}), bf16[16,2,128,512]{3,2,1,0:T(8,128)(2,1)}, u32[]{:S(2)}, u32[]{:S(2)}) async-start(bf16[16,2,128,512]{3,2,1,0:T(8,128)(2,1)} %bitcast.100), calls=%async_computation.1 | async-start | bytes 8388608 | tf_op jit(solution)/shard_map/all_to_all | solution.py:90
  127.7 36.7 %while.30 = (s32[]{:T(128)}, f32[128,4,8]{0,2,1:T(8,128)S(1)}, f32[128,4,8]{0,2,1:T(8,128)S(1)}, f32[128,4,8,128]{0,3,2,1:T(8,128)}, pred[2,128,512]{1,2,0:T(8,1...) while((s32[]{:T(128)}, f32[128,4,8]{0,2,1:T(8,128)S(1)}, ...), condition=%wide.region_3.4_spmd.clone, body=%wide.region_0.0_spmd.clone.sunk | while | flops 1106792448 | bytes 35192952 | solution.py:47
  129.3 4.6 %fusion.31 = (f32[128,4,8]{0,2,1:T(8,128)S(1)}, f32[4,512,128,8]{2,1,3,0:T(8,128)}) fusion(pred[128,512]{0,1:T(8,128)(4,1)S(1)} %dynamic-slice_bitcast_fusion.4, bf16[128,4,8,128]{3,0,2,1:T(8,128)(2,1)S(1)} %get-tuple-element.419, bf16[1,512,4,128]{3,2,1,0:T(4,128)(2,1)S(1)} %get-tuple-element.341), kind=kOutput, calls=%fused_computation.5.clone.1 | convolution fusion | flops 543158272 | bytes 10043392 | tf_op jit(solution)/shard_map/while/body/eval_jaxpr/swxl,cwl->swxc/dot_general | solution.py:29
  133.9 4.5 %convert_reduce_fusion.6 = f32[128,4,8]{0,2,1:T(8,128)S(1)} fusion(f32[128,4,8]{0,2,1:T(8,128)S(1)} %select_maximum_fusion.4, f32[4,512,128,8]{2,1,3,0:T(8,128)} %get-tuple-element.343, pred[128,512]{0,1:T(8,128)(4,1)S(1)} %dynamic-slice_bitcast_fusion.4), kind=kLoop, calls=%fused_computation.3.clone.1 | loop fusion | flops 14675968 | bytes 8486912 | tf_op jit(solution)/shard_map/while/body/eval_jaxpr/reduce_sum | solution.py:41
  138.7 7.0 %bitcast_add_fusion.4 = f32[128,4,8,128]{0,3,2,1:T(8,128)} fusion(f32[128,4,8,128]{0,3,2,1:T(8,128)} %get-tuple-element.406, f32[128,4,8]{0,2,1:T(8,128)S(1)} %get-tuple-element.345, pred[]{:T(512)S(6)} %compare.6, bf16[1,512,4,128]{1,3,2,0:T(8,128)(2,1)S(1)} %copy.60, f32[4,512,128,8]{2,1,3,0:T(8,128)} %get-tuple-element.343, ...), kind=kOutput, calls=%fused_computation.6.clone.1 | convolution fusion | flops 548929536 | bytes 13205505 | tf_op jit(solution)/shard_map/while/body/eval_jaxpr/unqy,ynx->unqx/dot_general | solution.py:42
  147.3 4.6 %fusion.31 = (f32[128,4,8]{0,2,1:T(8,128)S(1)}, f32[4,512,128,8]{2,1,3,0:T(8,128)}) fusion(pred[128,512]{0,1:T(8,128)(4,1)S(1)} %dynamic-slice_bitcast_fusion.4, bf16[128,4,8,128]{3,0,2,1:T(8,128)(2,1)S(1)} %get-tuple-element.419, bf16[1,512,4,128]{3,2,1,0:T(4,128)(2,1)S(1)} %get-tuple-element.341), kind=kOutput, calls=%fused_computation.5.clone.1 | convolution fusion | flops 543158272 | bytes 10043392 | tf_op jit(solution)/shard_map/while/body/eval_jaxpr/swxl,cwl->swxc/dot_general | solution.py:29
  151.9 4.5 %convert_reduce_fusion.6 = f32[128,4,8]{0,2,1:T(8,128)S(1)} fusion(f32[128,4,8]{0,2,1:T(8,128)S(1)} %select_maximum_fusion.4, f32[4,512,128,8]{2,1,3,0:T(8,128)} %get-tuple-element.343, pred[128,512]{0,1:T(8,128)(4,1)S(1)} %dynamic-slice_bitcast_fusion.4), kind=kLoop, calls=%fused_computation.3.clone.1 | loop fusion | flops 14675968 | bytes 8486912 | tf_op jit(solution)/shard_map/while/body/eval_jaxpr/reduce_sum | solution.py:41
  156.8 7.6 %bitcast_add_fusion.4 = f32[128,4,8,128]{0,3,2,1:T(8,128)} fusion(f32[128,4,8,128]{0,3,2,1:T(8,128)} %get-tuple-element.406, f32[128,4,8]{0,2,1:T(8,128)S(1)} %get-tuple-element.345, pred[]{:T(512)S(6)} %compare.6, bf16[1,512,4,128]{1,3,2,0:T(8,128)(2,1)S(1)} %copy.60, f32[4,512,128,8]{2,1,3,0:T(8,128)} %get-tuple-element.343, ...), kind=kOutput, calls=%fused_computation.6.clone.1 | convolution fusion | flops 548929536 | bytes 13205505 | tf_op jit(solution)/shard_map/while/body/eval_jaxpr/unqy,ynx->unqx/dot_general | solution.py:42
  164.4 7.0 %reshape_reshape.6 = bf16[8,512,4,128]{3,2,1,0:T(4,128)(2,1)} reshape(bf16[16,2,128,512]{3,2,1,0:T(8,128)(2,1)} %all-to-all-done) | data formatting | bytes 8388608 | tf_op jit(solution)/shard_map/reshape;reshape | solution.py:21
  171.3 18.5 %all-to-all-done.1 = bf16[16,2,128,512]{3,2,1,0:T(8,128)(2,1)} async-done(((bf16[16,2,128,512]{3,2,1,0:T(8,128)(2,1)}), bf16[16,2,128,512]{3,2,1,0:T(8,128)(2,1)}, u32[]{:S(2)}, u32[]{:S(2)}) %all-to-all-start.1) | async-done | bytes 4194336 | tf_op jit(solution)/shard_map/all_to_all | solution.py:90
  189.8 6.9 %reshape_reshape.7 = bf16[8,512,4,128]{3,2,1,0:T(4,128)(2,1)} reshape(bf16[16,2,128,512]{3,2,1,0:T(8,128)(2,1)} %all-to-all-done.1) | data formatting | bytes 8388608 | tf_op jit(solution)/shard_map/reshape;reshape | solution.py:22
  196.7 163.8 %while.31 = (s32[]{:T(128)}, f32[128,4,8]{0,2,1:T(8,128)S(1)}, f32[128,4,8]{0,2,1:T(8,128)S(1)}, f32[128,4,8,128]{0,3,2,1:T(8,128)}, pred[8,1,512]{2,1,0:T(4,128...) while((s32[]{:T(128)}, f32[128,4,8]{0,2,1:T(8,128)S(1)}, ...), condition=%wide.region_10.11_spmd.clone, body=%wide.region_7.10_spmd.clone.sunk | while | flops 1096306688 | bytes 51628208 | solution.py:47
  199.1 4.6 %bitcast_reduce_fusion.2 = (f32[128,4,8]{0,2,1:T(8,128)S(1)}, f32[4,512,128,8]{2,1,3,0:T(8,128)}) fusion(pred[512]{0:T(512)(128)(4,1)S(1)} %dynamic-slice_reduce_fusion.2, bf16[128,4,8,128]{3,0,2,1:T(8,128)(2,1)S(1)} %get-tuple-element.389, bf16[1,512,4,128]{3,2,1,0:T(4,128)(2,1)S(1)} %get-tuple-element.355), kind=kOutput, calls=%fused_computation.19.clone.1 | convolution fusion | flops 543158272 | bytes 9978368 | tf_op jit(solution)/shard_map/while/body/eval_jaxpr/swxl,cwl->swxc/dot_general | solution.py:29
  203.7 6.5 %convert_reduce_fusion.7 = (f32[128,4,8]{0,2,1:T(8,128)S(1)}, bf16[128,4,8,512]{0,3,2,1:T(8,128)(2,1)}) fusion(f32[128,4,8]{0,2,1:T(8,128)S(1)} %select_maximum_fusion.5, f32[4,512,128,8]{2,1,3,0:T(8,128)} %get-tuple-element.357, pred[512]{0:T(512)(128)(4,1)S(1)} %dynamic-slice_reduce_fusion.2), kind=kLoop, calls=%fused_computation.23.clone.1 | loop fusion | flops 14675968 | bytes 12616192 | tf_op jit(solution)/shard_map/while/body/eval_jaxpr/reduce_sum | solution.py:41
  219.6 4.6 %bitcast_reduce_fusion.2 = (f32[128,4,8]{0,2,1:T(8,128)S(1)}, f32[4,512,128,8]{2,1,3,0:T(8,128)}) fusion(pred[512]{0:T(512)(128)(4,1)S(1)} %dynamic-slice_reduce_fusion.2, bf16[128,4,8,128]{3,0,2,1:T(8,128)(2,1)S(1)} %get-tuple-element.389, bf16[1,512,4,128]{3,2,1,0:T(4,128)(2,1)S(1)} %get-tuple-element.355), kind=kOutput, calls=%fused_computation.19.clone.1 | convolution fusion | flops 543158272 | bytes 9978368 | tf_op jit(solution)/shard_map/while/body/eval_jaxpr/swxl,cwl->swxc/dot_general | solution.py:29
  224.2 6.5 %convert_reduce_fusion.7 = (f32[128,4,8]{0,2,1:T(8,128)S(1)}, bf16[128,4,8,512]{0,3,2,1:T(8,128)(2,1)}) fusion(f32[128,4,8]{0,2,1:T(8,128)S(1)} %select_maximum_fusion.5, f32[4,512,128,8]{2,1,3,0:T(8,128)} %get-tuple-element.357, pred[512]{0:T(512)(128)(4,1)S(1)} %dynamic-slice_reduce_fusion.2), kind=kLoop, calls=%fused_computation.23.clone.1 | loop fusion | flops 14675968 | bytes 12616192 | tf_op jit(solution)/shard_map/while/body/eval_jaxpr/reduce_sum | solution.py:41
  240.0 4.6 %bitcast_reduce_fusion.2 = (f32[128,4,8]{0,2,1:T(8,128)S(1)}, f32[4,512,128,8]{2,1,3,0:T(8,128)}) fusion(pred[512]{0:T(512)(128)(4,1)S(1)} %dynamic-slice_reduce_fusion.2, bf16[128,4,8,128]{3,0,2,1:T(8,128)(2,1)S(1)} %get-tuple-element.389, bf16[1,512,4,128]{3,2,1,0:T(4,128)(2,1)S(1)} %get-tuple-element.355), kind=kOutput, calls=%fused_computation.19.clone.1 | convolution fusion | flops 543158272 | bytes 9978368 | tf_op jit(solution)/shard_map/while/body/eval_jaxpr/swxl,cwl->swxc/dot_general | solution.py:29
  244.6 6.5 %convert_reduce_fusion.7 = (f32[128,4,8]{0,2,1:T(8,128)S(1)}, bf16[128,4,8,512]{0,3,2,1:T(8,128)(2,1)}) fusion(f32[128,4,8]{0,2,1:T(8,128)S(1)} %select_maximum_fusion.5, f32[4,512,128,8]{2,1,3,0:T(8,128)} %get-tuple-element.357, pred[512]{0:T(512)(128)(4,1)S(1)} %dynamic-slice_reduce_fusion.2), kind=kLoop, calls=%fused_computation.23.clone.1 | loop fusion | flops 14675968 | bytes 12616192 | tf_op jit(solution)/shard_map/while/body/eval_jaxpr/reduce_sum | solution.py:41
  260.5 4.6 %bitcast_reduce_fusion.2 = (f32[128,4,8]{0,2,1:T(8,128)S(1)}, f32[4,512,128,8]{2,1,3,0:T(8,128)}) fusion(pred[512]{0:T(512)(128)(4,1)S(1)} %dynamic-slice_reduce_fusion.2, bf16[128,4,8,128]{3,0,2,1:T(8,128)(2,1)S(1)} %get-tuple-element.389, bf16[1,512,4,128]{3,2,1,0:T(4,128)(2,1)S(1)} %get-tuple-element.355), kind=kOutput, calls=%fused_computation.19.clone.1 | convolution fusion | flops 543158272 | bytes 9978368 | tf_op jit(solution)/shard_map/while/body/eval_jaxpr/swxl,cwl->swxc/dot_general | solution.py:29
  265.1 6.5 %convert_reduce_fusion.7 = (f32[128,4,8]{0,2,1:T(8,128)S(1)}, bf16[128,4,8,512]{0,3,2,1:T(8,128)(2,1)}) fusion(f32[128,4,8]{0,2,1:T(8,128)S(1)} %select_maximum_fusion.5, f32[4,512,128,8]{2,1,3,0:T(8,128)} %get-tuple-element.357, pred[512]{0:T(512)(128)(4,1)S(1)} %dynamic-slice_reduce_fusion.2), kind=kLoop, calls=%fused_computation.23.clone.1 | loop fusion | flops 14675968 | bytes 12616192 | tf_op jit(solution)/shard_map/while/body/eval_jaxpr/reduce_sum | solution.py:41
  281.0 4.6 %bitcast_reduce_fusion.2 = (f32[128,4,8]{0,2,1:T(8,128)S(1)}, f32[4,512,128,8]{2,1,3,0:T(8,128)}) fusion(pred[512]{0:T(512)(128)(4,1)S(1)} %dynamic-slice_reduce_fusion.2, bf16[128,4,8,128]{3,0,2,1:T(8,128)(2,1)S(1)} %get-tuple-element.389, bf16[1,512,4,128]{3,2,1,0:T(4,128)(2,1)S(1)} %get-tuple-element.355), kind=kOutput, calls=%fused_computation.19.clone.1 | convolution fusion | flops 543158272 | bytes 9978368 | tf_op jit(solution)/shard_map/while/body/eval_jaxpr/swxl,cwl->swxc/dot_general | solution.py:29
  285.6 6.5 %convert_reduce_fusion.7 = (f32[128,4,8]{0,2,1:T(8,128)S(1)}, bf16[128,4,8,512]{0,3,2,1:T(8,128)(2,1)}) fusion(f32[128,4,8]{0,2,1:T(8,128)S(1)} %select_maximum_fusion.5, f32[4,512,128,8]{2,1,3,0:T(8,128)} %get-tuple-element.357, pred[512]{0:T(512)(128)(4,1)S(1)} %dynamic-slice_reduce_fusion.2), kind=kLoop, calls=%fused_computation.23.clone.1 | loop fusion | flops 14675968 | bytes 12616192 | tf_op jit(solution)/shard_map/while/body/eval_jaxpr/reduce_sum | solution.py:41
  301.5 4.6 %bitcast_reduce_fusion.2 = (f32[128,4,8]{0,2,1:T(8,128)S(1)}, f32[4,512,128,8]{2,1,3,0:T(8,128)}) fusion(pred[512]{0:T(512)(128)(4,1)S(1)} %dynamic-slice_reduce_fusion.2, bf16[128,4,8,128]{3,0,2,1:T(8,128)(2,1)S(1)} %get-tuple-element.389, bf16[1,512,4,128]{3,2,1,0:T(4,128)(2,1)S(1)} %get-tuple-element.355), kind=kOutput, calls=%fused_computation.19.clone.1 | convolution fusion | flops 543158272 | bytes 9978368 | tf_op jit(solution)/shard_map/while/body/eval_jaxpr/swxl,cwl->swxc/dot_general | solution.py:29
  306.0 6.5 %convert_reduce_fusion.7 = (f32[128,4,8]{0,2,1:T(8,128)S(1)}, bf16[128,4,8,512]{0,3,2,1:T(8,128)(2,1)}) fusion(f32[128,4,8]{0,2,1:T(8,128)S(1)} %select_maximum_fusion.5, f32[4,512,128,8]{2,1,3,0:T(8,128)} %get-tuple-element.357, pred[512]{0:T(512)(128)(4,1)S(1)} %dynamic-slice_reduce_fusion.2), kind=kLoop, calls=%fused_computation.23.clone.1 | loop fusion | flops 14675968 | bytes 12616192 | tf_op jit(solution)/shard_map/while/body/eval_jaxpr/reduce_sum | solution.py:41
  321.9 4.6 %bitcast_reduce_fusion.2 = (f32[128,4,8]{0,2,1:T(8,128)S(1)}, f32[4,512,128,8]{2,1,3,0:T(8,128)}) fusion(pred[512]{0:T(512)(128)(4,1)S(1)} %dynamic-slice_reduce_fusion.2, bf16[128,4,8,128]{3,0,2,1:T(8,128)(2,1)S(1)} %get-tuple-element.389, bf16[1,512,4,128]{3,2,1,0:T(4,128)(2,1)S(1)} %get-tuple-element.355), kind=kOutput, calls=%fused_computation.19.clone.1 | convolution fusion | flops 543158272 | bytes 9978368 | tf_op jit(solution)/shard_map/while/body/eval_jaxpr/swxl,cwl->swxc/dot_general | solution.py:29
  326.5 6.5 %convert_reduce_fusion.7 = (f32[128,4,8]{0,2,1:T(8,128)S(1)}, bf16[128,4,8,512]{0,3,2,1:T(8,128)(2,1)}) fusion(f32[128,4,8]{0,2,1:T(8,128)S(1)} %select_maximum_fusion.5, f32[4,512,128,8]{2,1,3,0:T(8,128)} %get-tuple-element.357, pred[512]{0:T(512)(128)(4,1)S(1)} %dynamic-slice_reduce_fusion.2), kind=kLoop, calls=%fused_computation.23.clone.1 | loop fusion | flops 14675968 | bytes 12616192 | tf_op jit(solution)/shard_map/while/body/eval_jaxpr/reduce_sum | solution.py:41
  342.4 4.6 %bitcast_reduce_fusion.2 = (f32[128,4,8]{0,2,1:T(8,128)S(1)}, f32[4,512,128,8]{2,1,3,0:T(8,128)}) fusion(pred[512]{0:T(512)(128)(4,1)S(1)} %dynamic-slice_reduce_fusion.2, bf16[128,4,8,128]{3,0,2,1:T(8,128)(2,1)S(1)} %get-tuple-element.389, bf16[1,512,4,128]{3,2,1,0:T(4,128)(2,1)S(1)} %get-tuple-element.355), kind=kOutput, calls=%fused_computation.19.clone.1 | convolution fusion | flops 543158272 | bytes 9978368 | tf_op jit(solution)/shard_map/while/body/eval_jaxpr/swxl,cwl->swxc/dot_general | solution.py:29
  347.0 6.5 %convert_reduce_fusion.7 = (f32[128,4,8]{0,2,1:T(8,128)S(1)}, bf16[128,4,8,512]{0,3,2,1:T(8,128)(2,1)}) fusion(f32[128,4,8]{0,2,1:T(8,128)S(1)} %select_maximum_fusion.5, f32[4,512,128,8]{2,1,3,0:T(8,128)} %get-tuple-element.357, pred[512]{0:T(512)(128)(4,1)S(1)} %dynamic-slice_reduce_fusion.2), kind=kLoop, calls=%fused_computation.23.clone.1 | loop fusion | flops 14675968 | bytes 12616192 | tf_op jit(solution)/shard_map/while/body/eval_jaxpr/reduce_sum | solution.py:41
  360.5 4.5 %add_divide_fusion = f32[128,4,8,128]{0,3,2,1:T(8,128)} fusion(f32[128,4,8,128]{0,3,2,1:T(8,128)} %get-tuple-element.96, f32[128,4,8,128]{0,3,2,1:T(8,128)} %get-tuple-element.93, f32[128,4,8]{0,2,1:T(8,128)S(1)} %get-tuple-element.223, f32[128,4,8]{0,2,1:T(8,128)S(1)} %get-tuple-element.225, f32[128,4,8]{0,2,1:T(8,128)S(1)} %get-tuple-element.224), kind=kLoop, calls=%fused_computation.37 | loop fusion | flops 2097152 | bytes 6340608 | tf_op jit(solution)/shard_map/div | solution.py:108
  (143 shorter events, 98.1 us)
Async XLA Ops:
  6.5 2.5 copy-start
  11.8 7.9 %copy-start.4 = (bf16[24,128,512]{2,1,0:T(8,128)(2,1)S(1)}, bf16[24,128,512]{2,1,0:T(8,128)(2,1)}, u32[]{:S(2)}) copy-start(bf16[24,128,512]{2,1,0:T(8,128)(2,1)} %param.15) | copy-start | bytes 9437188
  11.8 108.3 %all-to-all-start = ((bf16[16,2,128,512]{3,2,1,0:T(8,128)(2,1)}), bf16[16,2,128,512]{3,2,1,0:T(8,128)(2,1)}, u32[]{:S(2)}, u32[]{:S(2)}) async-start(bf16[16,2,128,512]{3,2,1,0:T(8,128)(2,1)} %bitcast.101), calls=%async_computation | async-start | bytes 8388608 | tf_op jit(solution)/shard_map/all_to_all | solution.py:89
  17.8 54.1 %all-gather.5.cloned.1.call-start = ((), (), s32[]{:S(2)}) async-start(), calls=%async_computation.3 | async-start | bytes 1179648 | tf_op jit(solution)/shard_map/all_gather | solution.py:83
  18.5 99.5 %all-gather.3.cloned.1.call-start = ((), (), s32[]{:S(2)}) async-start(), calls=%async_computation.2 | async-start | bytes 1179648 | tf_op jit(solution)/shard_map/all_gather | solution.py:82
  120.2 69.6 %all-to-all-start.1 = ((bf16[16,2,128,512]{3,2,1,0:T(8,128)(2,1)}), bf16[16,2,128,512]{3,2,1,0:T(8,128)(2,1)}, u32[]{:S(2)}, u32[]{:S(2)}) async-start(bf16[16,2,128,512]{3,2,1,0:T(8,128)(2,1)} %bitcast.100), calls=%async_computation.1 | async-start | bytes 8388608 | tf_op jit(solution)/shard_map/all_to_all | solution.py:90
  203.7 8.6 %copy-start.2 = (f32[128,4,8,128]{0,3,2,1:T(8,128)S(1)}, f32[128,4,8,128]{0,3,2,1:T(8,128)}, u32[]{:S(2)}) copy-start(f32[128,4,8,128]{0,3,2,1:T(8,128)} %get-tuple-element.376) | copy-start | bytes 6291460 | tf_op jit(solution)/shard_map/while
  215.9 1.3 copy-start.3
  224.2 8.6 %copy-start.2 = (f32[128,4,8,128]{0,3,2,1:T(8,128)S(1)}, f32[128,4,8,128]{0,3,2,1:T(8,128)}, u32[]{:S(2)}) copy-start(f32[128,4,8,128]{0,3,2,1:T(8,128)} %get-tuple-element.376) | copy-start | bytes 6291460 | tf_op jit(solution)/shard_map/while
  236.3 1.3 copy-start.3
  244.6 8.6 %copy-start.2 = (f32[128,4,8,128]{0,3,2,1:T(8,128)S(1)}, f32[128,4,8,128]{0,3,2,1:T(8,128)}, u32[]{:S(2)}) copy-start(f32[128,4,8,128]{0,3,2,1:T(8,128)} %get-tuple-element.376) | copy-start | bytes 6291460 | tf_op jit(solution)/shard_map/while
  256.8 1.3 copy-start.3
  265.1 8.6 %copy-start.2 = (f32[128,4,8,128]{0,3,2,1:T(8,128)S(1)}, f32[128,4,8,128]{0,3,2,1:T(8,128)}, u32[]{:S(2)}) copy-start(f32[128,4,8,128]{0,3,2,1:T(8,128)} %get-tuple-element.376) | copy-start | bytes 6291460 | tf_op jit(solution)/shard_map/while
  277.3 1.3 copy-start.3
  285.6 8.6 %copy-start.2 = (f32[128,4,8,128]{0,3,2,1:T(8,128)S(1)}, f32[128,4,8,128]{0,3,2,1:T(8,128)}, u32[]{:S(2)}) copy-start(f32[128,4,8,128]{0,3,2,1:T(8,128)} %get-tuple-element.376) | copy-start | bytes 6291460 | tf_op jit(solution)/shard_map/while
  297.8 1.3 copy-start.3
  306.0 8.6 %copy-start.2 = (f32[128,4,8,128]{0,3,2,1:T(8,128)S(1)}, f32[128,4,8,128]{0,3,2,1:T(8,128)}, u32[]{:S(2)}) copy-start(f32[128,4,8,128]{0,3,2,1:T(8,128)} %get-tuple-element.376) | copy-start | bytes 6291460 | tf_op jit(solution)/shard_map/while
  318.2 1.3 copy-start.3
  326.5 8.6 %copy-start.2 = (f32[128,4,8,128]{0,3,2,1:T(8,128)S(1)}, f32[128,4,8,128]{0,3,2,1:T(8,128)}, u32[]{:S(2)}) copy-start(f32[128,4,8,128]{0,3,2,1:T(8,128)} %get-tuple-element.376) | copy-start | bytes 6291460 | tf_op jit(solution)/shard_map/while
  338.7 1.3 copy-start.3
  347.0 8.6 %copy-start.2 = (f32[128,4,8,128]{0,3,2,1:T(8,128)S(1)}, f32[128,4,8,128]{0,3,2,1:T(8,128)}, u32[]{:S(2)}) copy-start(f32[128,4,8,128]{0,3,2,1:T(8,128)} %get-tuple-element.376) | copy-start | bytes 6291460 | tf_op jit(solution)/shard_map/while
  359.2 1.3 copy-start.3
  360.5 7.4 %copy-start.1 = (bf16[24,128,512]{2,1,0:T(8,128)(2,1)S(1)}, bf16[24,128,512]{2,1,0:T(8,128)(2,1)}, u32[]{:S(2)}) copy-start(bf16[24,128,512]{2,1,0:T(8,128)(2,1)} %param.14) | copy-start | bytes 9437188
Sparse Core Ops, SparseCore 0:
  21.0 50.8 all-gather.4
  74.2 43.7 all-gather.2
where the time goes:
time: 376 us; the launch traced here: 375 us
  waiting for transfers between devices  111 us (30%)
  matrix products  88.7 us (24%)
  local copies, waits for them, and re-layouts  79.4 us (21%)
  other arithmetic  68.5 us (18%)
  starting transfers between devices  13.6 us (4%)
  between operations  13.6 us (4%)
    reduce_sum x10, other arithmetic, block_step(): jnp.sum(softmax_weights, axis=-1, dtype=jnp.float32)  61 us
    all_gather x1, waiting for transfers between devices, body(): value_piece = lax.all_gather(span_values, 'cp', axis=1, tiled=True)  46.9 us
    dot_general x10, matrix products, block_step(): jnp.einsum('swxl,cwl->swxc', queries_grouped4, key_tile, preferred_elemen...  45.8 us
    all_gather x1, waiting for transfers between devices, body(): key_piece = lax.all_gather(span_keys, 'cp', axis=1, tiled=True)  44 us
    dot_general x10, matrix products, block_step(): jnp.einsum('unqy,ynx->unqx', softmax_weights, value_tile, preferred_eleme...  42.9 us
    dynamic_slice x28, local copies, waits for them, and re-layouts, attend(): lax.scan(block_step, running, (key_blocks, value_blocks, vis_blocks))[0]  39.7 us
    all_to_all x1, waiting for transfers between devices, body(): lax.all_to_all(pool_values[local_pages], 'pool', split_axis=0, concat_axi...  18.5 us
    while x42, local copies, waits for them, and re-layouts  10.5 us
  transfers between devices with their start and end apart: 4, of which 3 were waited for; matrix products, arithmetic and copies ran while one was open for 14% of the time, Pallas kernels for 0%

commit v1 on v0

v1 whole, which is shorter than its diff:
```python
import functools

import jax
import jax.numpy as jnp
import numpy as np
from jax import lax
from jax.experimental import pallas as pl
from jax.experimental.pallas import tpu as pltpu
from jax.sharding import PartitionSpec as P

HEAD_DIM = 128
HEADS = 32
KV_HEADS = 4
PAGES_DEV = 24
SLOTS = 32
TOK = 128
GROUPS = HEADS // KV_HEADS
COLS = GROUPS * HEAD_DIM

ROWS = 512
KEYS = 1024
VROWS = 144
NEG = -1e30
SCALE2 = float(HEAD_DIM**-0.5 * np.log2(np.e))
MESH = pl.DeviceIdType.MESH

CHUNK_OWNERS = ((0, 1, 2, 6), (3, 7, 8, 9), (10, 11, 14, 15), (4, 5, 12, 13))
SEND_ORDER = (1, 2, 6, 8, 3, 7, 9, 10, 14, 11, 15, 4, 12, 5, 13)
BLOCK_XOR = (0, 1, 3, 2)
BF16 = jnp.bfloat16
F32 = jnp.float32


def xor(index, offset):
    for bit in range(4):
        if offset >> bit & 1:
            index = index + (1 << bit) * (1 - 2 * ((index // (1 << bit)) % 2))
    return index


def schedule(u):
    chunk = jnp.where(u < 6, u // 3, jnp.where(u < 8, u - 6, u // 4))
    block = jnp.where(u < 6, u % 3, jnp.where(u < 8, 3, jnp.where(u < 16, u % 4, 3 - u % 4)))
    return chunk, block


def kernel(
    pid, npages, ids_ref, q_ref, sk_ref, sv_ref, pk_ref, pv_ref,
    out_ref, own_ref,
    pgs, pool_v, send_v, kv_v, qbuf, span_v, qaug, kaug, vt, m_ref, acc, s0, s1, x0, x1, obuf, own_v,
    loc_sem, q_send, q_recv, sp_send, sp_recv, pl_send, pl_recv, o_send, o_recv,
):
    me = lax.axis_index("pool")
    ctx = lax.axis_index("cp")
    head = ctx % 4
    my_cols = pl.ds(pl.multiple_of(head * HEAD_DIM, HEAD_DIM), HEAD_DIM)

    def group_cols(index):
        return pl.ds(pl.multiple_of(index * COLS, COLS), COLS)

    local = [
        pltpu.make_async_copy(pk_ref.at[:, :, my_cols], pool_v.at[0], loc_sem.at[0]),
        pltpu.make_async_copy(pv_ref.at[:, :, my_cols], pool_v.at[1], loc_sem.at[1]),
        pltpu.make_async_copy(q_ref.at[0, :, group_cols(head)], qbuf.at[0], loc_sem.at[2]),
        pltpu.make_async_copy(sk_ref.at[0, :, my_cols], span_v.at[0, 0], loc_sem.at[3]),
        pltpu.make_async_copy(sv_ref.at[0, :, my_cols], span_v.at[0, 1], loc_sem.at[4]),
    ]
    for copy in local:
        copy.start()

    barrier = pltpu.get_barrier_semaphore()
    for k in range(1, 16):
        pl.semaphore_signal(barrier, inc=1, device_id=(xor(me, k), ctx), device_id_type=MESH)
    for k in range(1, 8):
        pl.semaphore_signal(barrier, inc=1, device_id=(me, xor(ctx, k)), device_id_type=MESH)

    base = me * PAGES_DEV

    def scan(r, _):
        live = npages[r]
        first = jnp.int32(0)
        second = jnp.int32(0)
        for s in range(SLOTS):
            page = pid[r, s] - base
            hit = (page >= 0) & (page < PAGES_DEV) & (s < live)
            second = jnp.where(hit, first, second)
            first = jnp.where(hit, page, first)
        pgs[r, 0] = first
        pgs[r, 1] = second
        return 0

    lax.fori_loop(0, 16, scan, 0)
    pl.semaphore_wait(barrier, 22)

    q_copies = {}
    for slot in (1, 2, 3):
        mate = xor(ctx, BLOCK_XOR[slot])
        q_copies[slot] = pltpu.make_async_remote_copy(
            src_ref=q_ref.at[0, :, group_cols(mate % 4)], dst_ref=qbuf.at[slot],
            send_sem=q_send.at[slot], recv_sem=q_recv.at[slot],
            device_id=(me, mate), device_id_type=MESH)
        q_copies[slot].start()

    local[0].wait()
    local[1].wait()

    def pick(k, dst):
        r = xor(me, k)
        for cap in range(2):
            page = pgs[r, cap]
            dst[k, 0, cap] = pool_v[0, page]
            dst[k, 1, cap] = pool_v[1, page]

    pool_copies = {}
    for k in SEND_ORDER:
        pool_copies[k] = pltpu.make_async_remote_copy(
            src_ref=send_v.at[k], dst_ref=kv_v.at[k],
            send_sem=pl_send.at[k], recv_sem=pl_recv.at[k],
            device_id=(xor(me, k), ctx), device_id_type=MESH)
    pick(SEND_ORDER[0], send_v)
    for now, after in zip(SEND_ORDER, SEND_ORDER[1:] + (None,)):
        if after is not None:
            pick(after, send_v)
        else:
            pick(0, kv_v)
        pool_copies[now].start()

    span_copies = {}
    for k in (1, 3, 2, 4, 5, 7, 6):
        mate = xor(ctx, k)
        cols = pl.ds(pl.multiple_of((mate % 4) * HEAD_DIM, HEAD_DIM), HEAD_DIM)
        for which, ref in ((0, sk_ref), (1, sv_ref)):
            span_copies[k, which] = pltpu.make_async_remote_copy(
                src_ref=ref.at[0, :, cols], dst_ref=span_v.at[k, which],
                send_sem=sp_send.at[k, which], recv_sem=sp_recv.at[k, which],
                device_id=(me, mate), device_id_type=MESH)
            span_copies[k, which].start()

    row_iota = lax.broadcasted_iota(jnp.int32, (TOK, TOK), 0)
    col_iota = lax.broadcasted_iota(jnp.int32, (TOK, TOK), 1)
    eye = jnp.where(row_iota == col_iota, 1.0, 0.0).astype(F32).astype(BF16)
    later = jnp.where(row_iota > col_iota, NEG, 0.0).astype(F32).astype(BF16)
    for slot in range(4):
        for g in range(GROUPS):
            qaug[slot, g * TOK:(g + 1) * TOK, HEAD_DIM:] = eye
    for slot in range(4):
        for k in range(8):
            if BLOCK_XOR[slot] == k:
                mask = later
            else:
                hidden = xor(ctx, k) > xor(ctx, BLOCK_XOR[slot])
                mask = jnp.full((TOK, TOK), jnp.where(hidden, NEG, 0.0), F32).astype(BF16)
            kaug[4 + slot, k * TOK:(k + 1) * TOK, HEAD_DIM:] = mask
    my_ids = ids_ref[pl.ds(me, 1), :]
    slot_iota = lax.broadcasted_iota(jnp.int32, (1, SLOTS), 1)
    my_ids = jnp.where(slot_iota < npages[me], my_ids, -1)
    for j, owners in enumerate(CHUNK_OWNERS):
        for i, k in enumerate(owners):
            low = xor(me, k) * PAGES_DEV
            held = jnp.where((my_ids >= low) & (my_ids < low + PAGES_DEV), 1.0, 0.0).astype(F32)
            count = jnp.sum(held, axis=1, keepdims=True)
            for cap in range(2):
                bias = jnp.where(count > cap + 0.5, 0.0, NEG)
                at = (2 * i + cap) * TOK
                kaug[j, at:at + TOK, HEAD_DIM:] = jnp.broadcast_to(bias, (TOK, TOK)).astype(BF16)
    vt[:, HEAD_DIM:, :] = jnp.ones((5, VROWS - HEAD_DIM, KEYS), BF16)
    m_ref[...] = jnp.full(m_ref.shape, NEG, F32)
    acc[...] = jnp.zeros(acc.shape, F32)
    s1[...] = jnp.full(s1.shape, NEG, F32)
    x1[...] = jnp.full(x1.shape, NEG, F32)

    def load_block(slot):
        for g in range(GROUPS):
            qaug[slot, g * TOK:(g + 1) * TOK, :HEAD_DIM] = qbuf[slot, :, g * HEAD_DIM:(g + 1) * HEAD_DIM]

    def load_values(chunk, i, values):
        vt[chunk, :HEAD_DIM, i * TOK:(i + 1) * TOK] = values.astype(F32).T.astype(BF16)

    def load_prefix(j):
        for i, k in enumerate(CHUNK_OWNERS[j]):
            if k:
                pool_copies[k].wait_recv()
        for i, k in enumerate(CHUNK_OWNERS[j]):
            for cap in range(2):
                at = (2 * i + cap) * TOK
                kaug[j, at:at + TOK, :HEAD_DIM] = kv_v[k, 0, cap]
                load_values(j + (j > 1), 2 * i + cap, kv_v[k, 1, cap])

    def load_span():
        local[3].wait()
        local[4].wait()
        for k in range(1, 8):
            span_copies[k, 0].wait_recv()
            span_copies[k, 1].wait_recv()
        for k in range(8):
            for slot in range(4):
                kaug[4 + slot, k * TOK:(k + 1) * TOK, :HEAD_DIM] = span_v[k, 0]
            load_values(2, k, span_v[k, 1])

    def scores(chunk, block, half, s_ref, x_ref):
        at = jnp.where(chunk == 2, 4 + block, jnp.where(chunk > 2, chunk - 1, chunk))
        s = lax.dot_general(
            kaug[at], qaug[block, half * ROWS:(half + 1) * ROWS, :],
            (((1,), (1,)), ((), ())), preferred_element_type=F32)
        s_ref[...] = s
        x_ref[...] = jnp.max(s, axis=0, keepdims=True)

    def absorb(chunk, block, half, s_ref, x_ref):
        t = block * 2 + half
        m_old = m_ref[t]
        m_new = jnp.maximum(m_old, x_ref[...])
        alpha = jnp.exp2((m_old - m_new) * SCALE2)
        p = jnp.exp2((s_ref[...] - m_new) * SCALE2).astype(BF16)
        m_ref[t] = m_new
        acc[t] = acc[t] * alpha + jnp.dot(vt[chunk], p, preferred_element_type=F32)

    def body(now, before):
        scores(*now, 0, s0, x0)
        absorb(*before, 1, s1, x1)
        scores(*now, 1, s1, x1)
        absorb(*now, 0, s0, x0)

    def result(block, g):
        a = acc.at[block * 2 + g // 4]
        cols = slice(g % 4 * TOK, (g % 4 + 1) * TOK)
        return (a[:HEAD_DIM, cols] / a[HEAD_DIM:HEAD_DIM + 1, cols]).T

    local[2].wait()
    load_block(0)
    load_prefix(0)

    def step(u, _):
        for at, slot in ((1, 1), (2, 2), (6, 3)):
            @pl.when(u == at)
            def _():
                q_copies[slot].wait_recv()
                load_block(slot)

        @pl.when(u == 3)
        def _():
            load_prefix(1)

        @pl.when(u == 8)
        def _():
            load_span()

        @pl.when(u == 12)
        def _():
            load_prefix(2)

        @pl.when(u == 16)
        def _():
            load_prefix(3)

        body(schedule(u), schedule(jnp.maximum(u - 1, 0)))
        return 0

    lax.fori_loop(0, 17, step, 0)

    o_copies = []
    for block in (3, 2, 1):
        body((4, block - 1), (4, block))
        for g in range(GROUPS):
            obuf[block, :, g * HEAD_DIM:(g + 1) * HEAD_DIM] = result(block, g).astype(BF16)
        mate = xor(ctx, BLOCK_XOR[block])
        copy = pltpu.make_async_remote_copy(
            src_ref=obuf.at[block], dst_ref=out_ref.at[:, group_cols(head)],
            send_sem=o_send.at[block], recv_sem=o_recv.at[block],
            device_id=(me, mate), device_id_type=MESH)
        copy.start()
        o_copies.append(copy)
    absorb(4, 0, 1, s1, x1)
    for g in range(GROUPS):
        own_v[:, g * HEAD_DIM:(g + 1) * HEAD_DIM] = result(0, g)
    own_copy = pltpu.make_async_copy(own_v, own_ref, loc_sem.at[5])
    own_copy.start()

    for copies in (q_copies.values(), span_copies.values(), pool_copies.values()):
        for copy in copies:
            copy.wait_send()
    for copy in o_copies:
        copy.wait()
    own_copy.wait()


def attend(queries, span_keys, span_values, pool_keys, pool_values, page_ids, prefix_pages):
    vmem = pl.BlockSpec(memory_space=pltpu.VMEM)
    smem = pl.BlockSpec(memory_space=pltpu.SMEM)
    hbm = pl.BlockSpec(memory_space=pl.ANY)
    dma = pltpu.SemaphoreType.DMA
    far, own = pl.pallas_call(
        kernel,
        out_shape=(
            jax.ShapeDtypeStruct((TOK, HEADS * HEAD_DIM), BF16),
            jax.ShapeDtypeStruct((TOK, COLS), F32),
        ),
        in_specs=[smem, smem, vmem, hbm, hbm, hbm, hbm, hbm],
        out_specs=(hbm, hbm),
        scratch_shapes=[
            pltpu.SMEM((16, 2), jnp.int32),
            pltpu.VMEM((2, PAGES_DEV, TOK, HEAD_DIM), BF16),
            pltpu.VMEM((16, 2, 2, TOK, HEAD_DIM), BF16),
            pltpu.VMEM((16, 2, 2, TOK, HEAD_DIM), BF16),
            pltpu.VMEM((4, TOK, COLS), BF16),
            pltpu.VMEM((8, 2, TOK, HEAD_DIM), BF16),
            pltpu.VMEM((4, GROUPS * TOK, 2 * HEAD_DIM), BF16),
            pltpu.VMEM((8, KEYS, 2 * HEAD_DIM), BF16),
            pltpu.VMEM((5, VROWS, KEYS), BF16),
            pltpu.VMEM((8, 1, ROWS), F32),
            pltpu.VMEM((8, VROWS, ROWS), F32),
            pltpu.VMEM((KEYS, ROWS), F32),
            pltpu.VMEM((KEYS, ROWS), F32),
            pltpu.VMEM((1, ROWS), F32),
            pltpu.VMEM((1, ROWS), F32),
            pltpu.VMEM((4, TOK, COLS), BF16),
            pltpu.VMEM((TOK, COLS), F32),
            dma((6,)),
            dma((4,)), dma((4,)),
            dma((8, 2)), dma((8, 2)),
            dma((16,)), dma((16,)),
            dma((4,)), dma((4,)),
        ],
        compiler_params=pltpu.CompilerParams(
            collective_id=0, has_side_effects=True, vmem_limit_bytes=64000 * 1024),
        name="attend",
    )(page_ids, prefix_pages, page_ids, queries, span_keys, span_values, pool_keys, pool_values)
    start = lax.axis_index("cp") % 4 * COLS
    attended = lax.dynamic_update_slice(far.astype(F32), own, (0, start))
    return attended[None]


def solution(mesh):
    in_specs = (
        P("pool", "cp", None),
        P("pool", "cp", None),
        P("pool", "cp", None),
        P("pool", None, None),
        P("pool", None, None),
        P(),
        P(),
    )
    out_specs = P("pool", "cp", None)
    return jax.shard_map(attend, mesh=mesh, in_specs=in_specs, out_specs=out_specs, check_vma=False)
```

time: 376 us -> 73.3 us (0.19)
  the two profiles are of different devices: /device:TPU:103 before, /device:TPU:1 now
where the time goes in v1:
time: 73.3 us; the launch traced here: 73.2 us
  Pallas kernels  69.5 us (95%)
  other arithmetic  2.81 us (4%)
  local copies, waits for them, and re-layouts  0.83 us (1%)
    pallas_call x1, Pallas kernels, attend(): pl.pallas_call(kernel, out_shape=(jax.ShapeDtypeStruct((TOK, HEADS * HEAD...  69.5 us
    broadcast_in_dim x1, other arithmetic, attend(): return attended[None]  2.81 us

profile of v1, /device:TPU:1, one launch (start us, length us, event | category | flops | bytes accessed | tf_op | source)
XLA Modules:
  0.0 73.2 jit_solution(13658337329777140786)
XLA Ops:
  0.0 69.5 %attend.1 = (bf16[128,4096]{1,0:T(8,128)(2,1)}, f32[128,1024]{1,0:T(8,128)}) custom-call(s32[16,32]{1,0:T(8,128)} %ids_ref.1, s32[16]{0:T(128)} %npages.1, s32[16,32]{1,0:T(8,128)} %ids_ref.1, bf16[1,128,4096]{2,1,0:T(8,128)(2,1)} %q_ref.1, bf16[1,128,512]{2,1,0:T(8,128)(2,1)} %sk_ref.1, bf16[1,128,512]{2,1,0:T(8,128)(2,1)} %sv_ref.1, ...), custom_call_target="tpu_custom_call" | custom-call | tf_op jit(solution)/shard_map/attend/pallas_call | solution.py:291
  69.5 0.0 copy-start
  69.5 2.8 %bitcast_convert_fusion = f32[1,128,4096]{2,1,0:T(8,128)} fusion(bf16[128,4096]{1,0:T(8,128)(2,1)} %get-tuple-element.7), kind=kLoop, calls=%fused_computation | loop fusion | flops 524288 | bytes 3145728 | tf_op jit(solution)/shard_map/broadcast_in_dim | solution.py:329
  72.3 0.0 copy-done
  72.3 0.8 %bitcast_dynamic-update-slice_fusion = f32[1,128,4096]{2,1,0:T(8,128)} fusion(f32[1,128,4096]{2,1,0:T(8,128)} %bitcast_convert_fusion, s32[]{:T(128)S(6)} %select_n.11, f32[128,1024]{1,0:T(8,128)S(1)} %copy-done), kind=kLoop, calls=%fused_computation.1 | loop fusion | bytes 1048580 | tf_op jit(solution)/shard_map/dynamic_update_slice | solution.py:328
Async XLA Ops:
  69.5 2.8 %copy-start = (f32[128,1024]{1,0:T(8,128)S(1)}, f32[128,1024]{1,0:T(8,128)}, u32[]{:S(2)}) copy-start(f32[128,1024]{1,0:T(8,128)} %get-tuple-element.8) | copy-start | bytes 1572868

commit v2 on v1

--- a/solution.py
+++ b/solution.py
@@ -25,10 +25,12 @@
 MESH = pl.DeviceIdType.MESH
 
 CHUNK_OWNERS = ((0, 1, 2, 6), (3, 7, 8, 9), (10, 11, 14, 15), (4, 5, 12, 13))
-SEND_ORDER = (1, 2, 6, 8, 3, 7, 9, 10, 14, 11, 15, 4, 12, 5, 13)
+WAVES = ((1, 2, 6, 8, 9), (3, 7, 10, 14), (11, 15), (4, 12, 5, 13))
+OTHER_X = (9, 11, 13, 15)
 BLOCK_XOR = (0, 1, 3, 2)
 BF16 = jnp.bfloat16
 F32 = jnp.float32
+SPAN, LAST = 3, 4
 
 
 def xor(index, offset):
@@ -38,9 +40,16 @@
     return index
 
 
+def xor_block(index, block):
+    low = jnp.where(block == 3, 0, 1)
+    high = jnp.where(block == 1, 0, 1)
+    index = index + low * (1 - 2 * (index % 2))
+    return index + 2 * high * (1 - 2 * ((index // 2) % 2))
+
+
 def schedule(u):
-    chunk = jnp.where(u < 6, u // 3, jnp.where(u < 8, u - 6, u // 4))
-    block = jnp.where(u < 6, u % 3, jnp.where(u < 8, 3, jnp.where(u < 16, u % 4, 3 - u % 4)))
+    chunk = jnp.where(u < 9, u // 3, u - 9)
+    block = jnp.where(u < 9, u % 3, 3)
     return chunk, block
 
 
@@ -69,8 +78,10 @@
         copy.start()
 
     barrier = pltpu.get_barrier_semaphore()
+    other = xor(ctx, 4)
     for k in range(1, 16):
-        pl.semaphore_signal(barrier, inc=1, device_id=(xor(me, k), ctx), device_id_type=MESH)
+        pl.semaphore_signal(
+            barrier, inc=1, device_id=(xor(me, k), other if k in OTHER_X else ctx), device_id_type=MESH)
     for k in range(1, 8):
         pl.semaphore_signal(barrier, inc=1, device_id=(me, xor(ctx, k)), device_id_type=MESH)
 
@@ -99,7 +110,8 @@
             src_ref=q_ref.at[0, :, group_cols(mate % 4)], dst_ref=qbuf.at[slot],
             send_sem=q_send.at[slot], recv_sem=q_recv.at[slot],
             device_id=(me, mate), device_id_type=MESH)
-        q_copies[slot].start()
+    q_copies[1].start()
+    q_copies[2].start()
 
     local[0].wait()
     local[1].wait()
@@ -112,21 +124,26 @@
             dst[k, 1, cap] = pool_v[1, page]
 
     pool_copies = {}
-    for k in SEND_ORDER:
+    for k in range(1, 16):
         pool_copies[k] = pltpu.make_async_remote_copy(
             src_ref=send_v.at[k], dst_ref=kv_v.at[k],
             send_sem=pl_send.at[k], recv_sem=pl_recv.at[k],
-            device_id=(xor(me, k), ctx), device_id_type=MESH)
-    pick(SEND_ORDER[0], send_v)
-    for now, after in zip(SEND_ORDER, SEND_ORDER[1:] + (None,)):
-        if after is not None:
-            pick(after, send_v)
-        else:
-            pick(0, kv_v)
-        pool_copies[now].start()
+            device_id=(xor(me, k), other if k in OTHER_X else ctx), device_id_type=MESH)
+
+    def send_pages(wave):
+        for k in WAVES[wave]:
+            pool_copies[k].start()
+
+    for k in WAVES[0]:
+        pick(k, send_v)
+    pick(0, kv_v)
+    send_pages(0)
+    for wave in WAVES[1:]:
+        for k in wave:
+            pick(k, send_v)
 
     span_copies = {}
-    for k in (1, 3, 2, 4, 5, 7, 6):
+    for k in range(1, 8):
         mate = xor(ctx, k)
         cols = pl.ds(pl.multiple_of((mate % 4) * HEAD_DIM, HEAD_DIM), HEAD_DIM)
         for which, ref in ((0, sk_ref), (1, sv_ref)):
@@ -134,7 +151,17 @@
                 src_ref=ref.at[0, :, cols], dst_ref=span_v.at[k, which],
                 send_sem=sp_send.at[k, which], recv_sem=sp_recv.at[k, which],
                 device_id=(me, mate), device_id_type=MESH)
-            span_copies[k, which].start()
+
+    def send_span():
+        for k in (1, 3, 2):
+            span_copies[k, 0].start()
+            span_copies[k, 1].start()
+
+        @pl.when(ctx < 4)
+        def _():
+            for k in (4, 5, 7, 6):
+                span_copies[k, 0].start()
+                span_copies[k, 1].start()
 
     row_iota = lax.broadcasted_iota(jnp.int32, (TOK, TOK), 0)
     col_iota = lax.broadcasted_iota(jnp.int32, (TOK, TOK), 1)
@@ -184,21 +211,31 @@
             for cap in range(2):
                 at = (2 * i + cap) * TOK
                 kaug[j, at:at + TOK, :HEAD_DIM] = kv_v[k, 0, cap]
-                load_values(j + (j > 1), 2 * i + cap, kv_v[k, 1, cap])
+                load_values(j + (j > 2), 2 * i + cap, kv_v[k, 1, cap])
 
     def load_span():
         local[3].wait()
         local[4].wait()
-        for k in range(1, 8):
+        for k in range(1, 4):
             span_copies[k, 0].wait_recv()
             span_copies[k, 1].wait_recv()
+
+        @pl.when(ctx >= 4)
+        def _():
+            for k in range(4, 8):
+                span_copies[k, 0].wait_recv()
+                span_copies[k, 1].wait_recv()
+
         for k in range(8):
+            at = jnp.where(ctx < 4, k % 4, k)
             for slot in range(4):
-                kaug[4 + slot, k * TOK:(k + 1) * TOK, :HEAD_DIM] = span_v[k, 0]
-            load_values(2, k, span_v[k, 1])
+                kaug[4 + slot, k * TOK:(k + 1) * TOK, :HEAD_DIM] = span_v[at, 0]
+            load_values(3, k, span_v[at, 1])
 
     def scores(chunk, block, half, s_ref, x_ref):
-        at = jnp.where(chunk == 2, 4 + block, jnp.where(chunk > 2, chunk - 1, chunk))
+        at = chunk
+        if isinstance(chunk, int) and chunk >= SPAN:
+            at = 4 + block if chunk == SPAN else 3
         s = lax.dot_general(
             kaug[at], qaug[block, half * ROWS:(half + 1) * ROWS, :],
             (((1,), (1,)), ((), ())), preferred_element_type=F32)
@@ -220,66 +257,105 @@
         scores(*now, 1, s1, x1)
         absorb(*now, 0, s0, x0)
 
-    def result(block, g):
-        a = acc.at[block * 2 + g // 4]
-        cols = slice(g % 4 * TOK, (g % 4 + 1) * TOK)
+    def result(block, half, g):
+        a = acc.at[block * 2 + half]
+        cols = slice(g * TOK, (g + 1) * TOK)
         return (a[:HEAD_DIM, cols] / a[HEAD_DIM:HEAD_DIM + 1, cols]).T
+
+    def out_copy(block, half):
+        mate = xor_block(ctx, block)
+        cols = pl.ds(pl.multiple_of(head * COLS + half * (COLS // 2), COLS // 2), COLS // 2)
+        return pltpu.make_async_remote_copy(
+            src_ref=obuf.at[block, half], dst_ref=out_ref.at[:, cols],
+            send_sem=o_send.at[block, half], recv_sem=o_recv.at[block, half],
+            device_id=(me, mate), device_id_type=MESH)
+
+    def send(block, half):
+        for g in range(4):
+            obuf[block, half, :, g * HEAD_DIM:(g + 1) * HEAD_DIM] = result(block, half, g).astype(BF16)
+        out_copy(block, half).start()
+
+    def keep(half):
+        for g in range(4):
+            at = (half * 4 + g) * HEAD_DIM
+            own_v[:, at:at + HEAD_DIM] = result(0, half, g)
 
     local[2].wait()
     load_block(0)
+    for k in WAVES[0]:
+        pool_copies[k].wait_send()
+    send_pages(1)
     load_prefix(0)
 
     def step(u, _):
-        for at, slot in ((1, 1), (2, 2), (6, 3)):
+        for at, slot in ((1, 1), (2, 2), (9, 3)):
             @pl.when(u == at)
             def _():
                 q_copies[slot].wait_recv()
                 load_block(slot)
 
+        for at, j in ((3, 1), (6, 2)):
+            @pl.when(u == at)
+            def _():
+                load_prefix(j)
+
+        @pl.when(u == 1)
+        def _():
+            send_pages(2)
+            q_copies[3].start()
+
+        @pl.when(u == 2)
+        def _():
+            send_span()
+
         @pl.when(u == 3)
         def _():
-            load_prefix(1)
-
-        @pl.when(u == 8)
-        def _():
-            load_span()
-
-        @pl.when(u == 12)
-        def _():
-            load_prefix(2)
-
-        @pl.when(u == 16)
-        def _():
-            load_prefix(3)
+            send_pages(3)
 
         body(schedule(u), schedule(jnp.maximum(u - 1, 0)))
         return 0
 
-    lax.fori_loop(0, 17, step, 0)
-
-    o_copies = []
-    for block in (3, 2, 1):
-        body((4, block - 1), (4, block))
-        for g in range(GROUPS):
-            obuf[block, :, g * HEAD_DIM:(g + 1) * HEAD_DIM] = result(block, g).astype(BF16)
-        mate = xor(ctx, BLOCK_XOR[block])
-        copy = pltpu.make_async_remote_copy(
-            src_ref=obuf.at[block], dst_ref=out_ref.at[:, group_cols(head)],
-            send_sem=o_send.at[block], recv_sem=o_recv.at[block],
-            device_id=(me, mate), device_id_type=MESH)
-        copy.start()
-        o_copies.append(copy)
-    absorb(4, 0, 1, s1, x1)
-    for g in range(GROUPS):
-        own_v[:, g * HEAD_DIM:(g + 1) * HEAD_DIM] = result(0, g)
+    lax.fori_loop(0, 12, step, 0)
+    load_span()
+    body((SPAN, 3), (2, 3))
+    body((SPAN, 2), (SPAN, 3))
+    load_prefix(3)
+    body((LAST, 3), (SPAN, 2))
+    send(3, 0)
+    body((LAST, 2), (LAST, 3))
+    send(3, 1)
+    send(2, 0)
+    body((SPAN, 1), (LAST, 2))
+    send(2, 1)
+    body((LAST, 1), (SPAN, 1))
+    send(1, 0)
+    body((SPAN, 0), (LAST, 1))
+    send(1, 1)
+    body((LAST, 0), (SPAN, 0))
+    keep(0)
+    absorb(LAST, 0, 1, s1, x1)
+    keep(1)
     own_copy = pltpu.make_async_copy(own_v, own_ref, loc_sem.at[5])
     own_copy.start()
 
-    for copies in (q_copies.values(), span_copies.values(), pool_copies.values()):
-        for copy in copies:
-            copy.wait_send()
-    for copy in o_copies:
-        copy.wait()
+    for slot in (1, 2, 3):
+        q_copies[slot].wait_send()
+    for wave in WAVES[1:]:
+        for k in wave:
+            pool_copies[k].wait_send()
+    for k in range(1, 4):
+        span_copies[k, 0].wait_send()
+        span_copies[k, 1].wait_send()
+
+    @pl.when(ctx < 4)
+    def _():
+        for k in range(4, 8):
+            span_copies[k, 0].wait_send()
+            span_copies[k, 1].wait_send()
+
+    for block in (3, 2, 1):
+        for half in range(2):
+            out_copy(block, half).wait()
     own_copy.wait()
 
 
@@ -312,13 +388,13 @@
             pltpu.VMEM((KEYS, ROWS), F32),
             pltpu.VMEM((1, ROWS), F32),
             pltpu.VMEM((1, ROWS), F32),
-            pltpu.VMEM((4, TOK, COLS), BF16),
+            pltpu.VMEM((4, 2, TOK, COLS // 2), BF16),
             pltpu.VMEM((TOK, COLS), F32),
             dma((6,)),
             dma((4,)), dma((4,)),
             dma((8, 2)), dma((8, 2)),
             dma((16,)), dma((16,)),
-            dma((4,)), dma((4,)),
+            dma((4, 2)), dma((4, 2)),
         ],
         compiler_params=pltpu.CompilerParams(
             collective_id=0, has_side_effects=True, vmem_limit_bytes=64000 * 1024),

time: 73.3 us -> 60.6 us (0.83)
  the two profiles are of different devices: /device:TPU:1 before, /device:TPU:103 now
where the time goes in v2:
time: 60.6 us; the launch traced here: 60.4 us
  Pallas kernels  56.7 us (94%)
  other arithmetic  2.81 us (5%)
  local copies, waits for them, and re-layouts  0.83 us (1%)
    pallas_call x1, Pallas kernels, attend(): pl.pallas_call(kernel, out_shape=(jax.ShapeDtypeStruct((TOK, HEADS * HEAD...  56.7 us
    broadcast_in_dim x1, other arithmetic, attend(): return attended[None]  2.81 us

profile of v2, /device:TPU:103, one launch (start us, length us, event | category | flops | bytes accessed | tf_op | source)
XLA Modules:
  0.0 60.4 jit_solution(1052456540166975446)
XLA Ops:
  0.0 56.7 %attend.1 = (bf16[128,4096]{1,0:T(8,128)(2,1)}, f32[128,1024]{1,0:T(8,128)}) custom-call(s32[16,32]{1,0:T(8,128)} %ids_ref.1, s32[16]{0:T(128)} %npages.1, s32[16,32]{1,0:T(8,128)} %ids_ref.1, bf16[1,128,4096]{2,1,0:T(8,128)(2,1)} %q_ref.1, bf16[1,128,512]{2,1,0:T(8,128)(2,1)} %sk_ref.1, bf16[1,128,512]{2,1,0:T(8,128)(2,1)} %sv_ref.1, ...), custom_call_target="tpu_custom_call" | custom-call | tf_op jit(solution)/shard_map/attend/pallas_call | solution.py:367
  56.7 0.0 copy-start
  56.7 2.8 %bitcast_convert_fusion = f32[1,128,4096]{2,1,0:T(8,128)} fusion(bf16[128,4096]{1,0:T(8,128)(2,1)} %get-tuple-element.7), kind=kLoop, calls=%fused_computation | loop fusion | flops 524288 | bytes 3145728 | tf_op jit(solution)/shard_map/broadcast_in_dim | solution.py:405
  59.5 0.0 copy-done
  59.5 0.8 %bitcast_dynamic-update-slice_fusion = f32[1,128,4096]{2,1,0:T(8,128)} fusion(f32[1,128,4096]{2,1,0:T(8,128)} %bitcast_convert_fusion, s32[]{:T(128)S(6)} %select_n.11, f32[128,1024]{1,0:T(8,128)S(1)} %copy-done), kind=kLoop, calls=%fused_computation.1 | loop fusion | bytes 1048580 | tf_op jit(solution)/shard_map/dynamic_update_slice | solution.py:404
Async XLA Ops:
  56.7 2.8 %copy-start = (f32[128,1024]{1,0:T(8,128)S(1)}, f32[128,1024]{1,0:T(8,128)}, u32[]{:S(2)}) copy-start(f32[128,1024]{1,0:T(8,128)} %get-tuple-element.8) | copy-start | bytes 1572868

commit v3 on v2

--- a/solution.py
+++ b/solution.py
@@ -24,13 +24,15 @@
 SCALE2 = float(HEAD_DIM**-0.5 * np.log2(np.e))
 MESH = pl.DeviceIdType.MESH
 
-CHUNK_OWNERS = ((0, 1, 2, 6), (3, 7, 8, 9), (10, 11, 14, 15), (4, 5, 12, 13))
-WAVES = ((1, 2, 6, 8, 9), (3, 7, 10, 14), (11, 15), (4, 12, 5, 13))
-OTHER_X = (9, 11, 13, 15)
+CHUNK_OWNERS = ((0, 1, 8, 9), (2, 3, 6, 7), (10, 11, 14, 15), (4, 5, 12, 13))
+WAVES = ((8, 9, 1, 2, 6, 3, 7), (4, 12), (10, 14, 11, 15))
+FAR = (4, 12)
+OTHER_X = (9, 11, 15)
 BLOCK_XOR = (0, 1, 3, 2)
 BF16 = jnp.bfloat16
 F32 = jnp.float32
 SPAN, LAST = 3, 4
+CONVERT_ROWS = 64
 
 
 def xor(index, offset):
@@ -48,8 +50,8 @@
 
 
 def schedule(u):
-    chunk = jnp.where(u < 9, u // 3, u - 9)
-    block = jnp.where(u < 9, u % 3, 3)
+    chunk = jnp.where(u < 6, u // 3, jnp.where(u < 8, u - 6, SPAN))
+    block = jnp.where(u < 6, u % 3, jnp.where(u < 8, 3, u - 8))
     return chunk, block
 
 
@@ -79,9 +81,19 @@
 
     barrier = pltpu.get_barrier_semaphore()
     other = xor(ctx, 4)
-    for k in range(1, 16):
-        pl.semaphore_signal(
-            barrier, inc=1, device_id=(xor(me, k), other if k in OTHER_X else ctx), device_id_type=MESH)
+    later_half = ctx // 4
+
+    def owner(k):
+        index = xor(me, k)
+        return index + later_half * (1 - 2 * (index % 2)) if k in FAR else index
+
+    def slot_of(k):
+        return k + later_half if k in FAR else k
+
+    for wave in WAVES:
+        for k in wave:
+            pl.semaphore_signal(
+                barrier, inc=1, device_id=(owner(k), other if k in OTHER_X else ctx), device_id_type=MESH)
     for k in range(1, 8):
         pl.semaphore_signal(barrier, inc=1, device_id=(me, xor(ctx, k)), device_id_type=MESH)
 
@@ -101,7 +113,7 @@
         return 0
 
     lax.fori_loop(0, 16, scan, 0)
-    pl.semaphore_wait(barrier, 22)
+    pl.semaphore_wait(barrier, sum(map(len, WAVES)) + 7)
 
     q_copies = {}
     for slot in (1, 2, 3):
@@ -117,18 +129,32 @@
     local[1].wait()
 
     def pick(k, dst):
-        r = xor(me, k)
+        r = owner(k)
+        slot = slot_of(k)
         for cap in range(2):
             page = pgs[r, cap]
-            dst[k, 0, cap] = pool_v[0, page]
-            dst[k, 1, cap] = pool_v[1, page]
+            dst[slot, 0, cap] = pool_v[0, page]
+            dst[slot, 1, cap] = pool_v[1, page]
 
     pool_copies = {}
-    for k in range(1, 16):
-        pool_copies[k] = pltpu.make_async_remote_copy(
-            src_ref=send_v.at[k], dst_ref=kv_v.at[k],
-            send_sem=pl_send.at[k], recv_sem=pl_recv.at[k],
-            device_id=(xor(me, k), other if k in OTHER_X else ctx), device_id_type=MESH)
+    for wave in WAVES:
+        for k in wave:
+            slot = slot_of(k)
+            pool_copies[k] = pltpu.make_async_remote_copy(
+                src_ref=send_v.at[slot], dst_ref=kv_v.at[slot],
+                send_sem=pl_send.at[slot], recv_sem=pl_recv.at[slot],
+                device_id=(owner(k), other if k in OTHER_X else ctx), device_id_type=MESH)
+
+    def passed_on(k, slot):
+        return pltpu.make_async_remote_copy(
+            src_ref=kv_v.at[slot], dst_ref=kv_v.at[slot],
+            send_sem=pl_send.at[2 * k + 1 - slot], recv_sem=pl_recv.at[slot],
+            device_id=(me, other), device_id_type=MESH)
+
+    def pass_on():
+        for k in FAR:
+            pool_copies[k].wait_recv()
+            passed_on(k, slot_of(k)).start()
 
     def send_pages(wave):
         for k in WAVES[wave]:
@@ -205,7 +231,9 @@
 
     def load_prefix(j):
         for i, k in enumerate(CHUNK_OWNERS[j]):
-            if k:
+            if k in FAR:
+                passed_on(k, k + 1 - later_half).wait_recv()
+            elif k and k - 1 not in FAR:
                 pool_copies[k].wait_recv()
         for i, k in enumerate(CHUNK_OWNERS[j]):
             for cap in range(2):
@@ -233,9 +261,10 @@
             load_values(3, k, span_v[at, 1])
 
     def scores(chunk, block, half, s_ref, x_ref):
-        at = chunk
-        if isinstance(chunk, int) and chunk >= SPAN:
-            at = 4 + block if chunk == SPAN else 3
+        if isinstance(chunk, int):
+            at = 3 if chunk == LAST else chunk
+        else:
+            at = jnp.where(chunk == SPAN, 4 + block, chunk)
         s = lax.dot_general(
             kaug[at], qaug[block, half * ROWS:(half + 1) * ROWS, :],
             (((1,), (1,)), ((), ())), preferred_element_type=F32)
@@ -282,56 +311,69 @@
 
     local[2].wait()
     load_block(0)
-    for k in WAVES[0]:
-        pool_copies[k].wait_send()
+    load_prefix(0)
     send_pages(1)
-    load_prefix(0)
 
     def step(u, _):
-        for at, slot in ((1, 1), (2, 2), (9, 3)):
+        @pl.when(u == 8)
+        def _():
+            pass_on()
+            load_span()
+
+        for at, slot in ((1, 1), (2, 2), (6, 3)):
             @pl.when(u == at)
             def _():
                 q_copies[slot].wait_recv()
                 load_block(slot)
 
-        for at, j in ((3, 1), (6, 2)):
-            @pl.when(u == at)
-            def _():
-                load_prefix(j)
+        @pl.when(u == 3)
+        def _():
+            load_prefix(1)
 
         @pl.when(u == 1)
         def _():
+            q_copies[3].start()
+
+        @pl.when(u == 2)
+        def _():
+            send_span()
+
+        @pl.when(u == 4)
+        def _():
             send_pages(2)
-            q_copies[3].start()
-
-        @pl.when(u == 2)
-        def _():
-            send_span()
-
-        @pl.when(u == 3)
-        def _():
-            send_pages(3)
 
         body(schedule(u), schedule(jnp.maximum(u - 1, 0)))
         return 0
 
     lax.fori_loop(0, 12, step, 0)
-    load_span()
-    body((SPAN, 3), (2, 3))
-    body((SPAN, 2), (SPAN, 3))
-    load_prefix(3)
-    body((LAST, 3), (SPAN, 2))
-    send(3, 0)
-    body((LAST, 2), (LAST, 3))
-    send(3, 1)
-    send(2, 0)
-    body((SPAN, 1), (LAST, 2))
-    send(2, 1)
-    body((LAST, 1), (SPAN, 1))
-    send(1, 0)
-    body((SPAN, 0), (LAST, 1))
-    send(1, 1)
-    body((LAST, 0), (SPAN, 0))
+
+    def finish(i, _):
+        block = 3 - i
+
+        @pl.when(i == 0)
+        def _():
+            load_prefix(2)
+
+        before = jnp.where(i == 0, SPAN, LAST)
+        body((2, block), (before, jnp.minimum(block + 1, 3)))
+
+        @pl.when(i > 0)
+        def _():
+            send(block + 1, 1)
+
+        @pl.when(i == 0)
+        def _():
+            load_prefix(3)
+
+        body((LAST, block), (2, block))
+
+        @pl.when(i < 3)
+        def _():
+            send(block, 0)
+
+        return 0
+
+    lax.fori_loop(0, 4, finish, 0)
     keep(0)
     absorb(LAST, 0, 1, s1, x1)
     keep(1)
@@ -340,9 +382,11 @@
 
     for slot in (1, 2, 3):
         q_copies[slot].wait_send()
-    for wave in WAVES[1:]:
+    for wave in WAVES:
         for k in wave:
             pool_copies[k].wait_send()
+    for k in FAR:
+        passed_on(k, slot_of(k)).wait_send()
     for k in range(1, 4):
         span_copies[k, 0].wait_send()
         span_copies[k, 1].wait_send()
@@ -400,9 +444,23 @@
             collective_id=0, has_side_effects=True, vmem_limit_bytes=64000 * 1024),
         name="attend",
     )(page_ids, prefix_pages, page_ids, queries, span_keys, span_values, pool_keys, pool_values)
-    start = lax.axis_index("cp") % 4 * COLS
-    attended = lax.dynamic_update_slice(far.astype(F32), own, (0, start))
-    return attended[None]
+    def convert(far_ref, own_ref, out_ref):
+        head = lax.axis_index("cp") % 4
+        out_ref[0] = far_ref[...].astype(F32)
+        cols = pl.ds(pl.multiple_of(head * COLS, COLS), COLS)
+        out_ref[0, :, cols] = own_ref[...]
+
+    return pl.pallas_call(
+        convert,
+        out_shape=jax.ShapeDtypeStruct((1, TOK, HEADS * HEAD_DIM), F32),
+        grid=(TOK // CONVERT_ROWS,),
+        in_specs=[
+            pl.BlockSpec((CONVERT_ROWS, HEADS * HEAD_DIM), lambda i: (i, 0)),
+            pl.BlockSpec((CONVERT_ROWS, COLS), lambda i: (i, 0)),
+        ],
+        out_specs=pl.BlockSpec((1, CONVERT_ROWS, HEADS * HEAD_DIM), lambda i: (0, i, 0)),
+        name="convert",
+    )(far, own)
 
 
 def solution(mesh):

time: 60.6 us -> 57 us (0.941)
  the two profiles are of different devices: /device:TPU:103 before, /device:TPU:7 now
where the time goes in v3:
time: 57 us; the launch traced here: 56.8 us
  Pallas kernels  56.8 us (100%)
    pallas_call x1, Pallas kernels, attend(): pl.pallas_call(kernel, out_shape=(jax.ShapeDtypeStruct((TOK, HEADS * HEAD...  54.3 us
    pallas_call x1, Pallas kernels, attend(): pl.pallas_call(convert, out_shape=jax.ShapeDtypeStruct((1, TOK, HEADS * H...  2.53 us

profile of v3, /device:TPU:7, one launch (start us, length us, event | category | flops | bytes accessed | tf_op | source)
XLA Modules:
  0.0 56.8 jit_solution(16903871465836370270)
XLA Ops:
  0.0 54.3 %attend.1 = (bf16[128,4096]{1,0:T(8,128)(2,1)}, f32[128,1024]{1,0:T(8,128)}) custom-call(s32[16,32]{1,0:T(8,128)} %ids_ref.1, s32[16]{0:T(128)} %npages.1, s32[16,32]{1,0:T(8,128)} %ids_ref.1, bf16[1,128,4096]{2,1,0:T(8,128)(2,1)} %q_ref.1, bf16[1,128,512]{2,1,0:T(8,128)(2,1)} %sk_ref.1, bf16[1,128,512]{2,1,0:T(8,128)(2,1)} %sv_ref.1, ...), custom_call_target="tpu_custom_call" | custom-call | tf_op jit(solution)/shard_map/attend/pallas_call | solution.py:411
  54.3 2.5 %convert.1 = f32[1,128,4096]{2,1,0:T(8,128)} custom-call(bf16[128,4096]{1,0:T(8,128)(2,1)} %get-tuple-element.7.far_ref, f32[128,1024]{1,0:T(8,128)} %get-tuple-element.8.own_ref), custom_call_target="tpu_custom_call" | custom-call | tf_op jit(solution)/shard_map/convert/pallas_call | solution.py:453

commit v4 on v3

--- a/solution.py
+++ b/solution.py
@@ -24,8 +24,8 @@
 SCALE2 = float(HEAD_DIM**-0.5 * np.log2(np.e))
 MESH = pl.DeviceIdType.MESH
 
-CHUNK_OWNERS = ((0, 1, 8, 9), (2, 3, 6, 7), (10, 11, 14, 15), (4, 5, 12, 13))
-WAVES = ((8, 9, 1, 2, 6, 3, 7), (4, 12), (10, 14, 11, 15))
+CHUNK_OWNERS = ((0, 1, 8, 9), (2, 6, 4, 12), (10, 11, 14, 15), (3, 7, 5, 13))
+WAVES = ((8, 9, 1, 4, 12), (2, 6), (10, 15), (14, 11), (3, 7))
 FAR = (4, 12)
 OTHER_X = (9, 11, 15)
 BLOCK_XOR = (0, 1, 3, 2)
@@ -50,8 +50,8 @@
 
 
 def schedule(u):
-    chunk = jnp.where(u < 6, u // 3, jnp.where(u < 8, u - 6, SPAN))
-    block = jnp.where(u < 6, u % 3, jnp.where(u < 8, 3, u - 8))
+    chunk = jnp.where(u < 6, u // 3, u - 6)
+    block = jnp.where(u < 6, u % 3, 3)
     return chunk, block
 
 
@@ -85,10 +85,14 @@
 
     def owner(k):
         index = xor(me, k)
-        return index + later_half * (1 - 2 * (index % 2)) if k in FAR else index
+        if k in FAR or k - 1 in FAR:
+            index = index + later_half * (1 - 2 * (index % 2))
+        return index
 
     def slot_of(k):
-        return k + later_half if k in FAR else k
+        if k in FAR:
+            return k + later_half
+        return k - later_half if k - 1 in FAR else k
 
     for wave in WAVES:
         for k in wave:
@@ -164,9 +168,6 @@
         pick(k, send_v)
     pick(0, kv_v)
     send_pages(0)
-    for wave in WAVES[1:]:
-        for k in wave:
-            pick(k, send_v)
 
     span_copies = {}
     for k in range(1, 8):
@@ -178,16 +179,14 @@
                 send_sem=sp_send.at[k, which], recv_sem=sp_recv.at[k, which],
                 device_id=(me, mate), device_id_type=MESH)
 
+    for wave in WAVES[1:]:
+        for k in wave:
+            pick(k, send_v)
+
     def send_span():
         for k in (1, 3, 2):
             span_copies[k, 0].start()
             span_copies[k, 1].start()
-
-        @pl.when(ctx < 4)
-        def _():
-            for k in (4, 5, 7, 6):
-                span_copies[k, 0].start()
-                span_copies[k, 1].start()
 
     row_iota = lax.broadcasted_iota(jnp.int32, (TOK, TOK), 0)
     col_iota = lax.broadcasted_iota(jnp.int32, (TOK, TOK), 1)
@@ -209,7 +208,7 @@
     my_ids = jnp.where(slot_iota < npages[me], my_ids, -1)
     for j, owners in enumerate(CHUNK_OWNERS):
         for i, k in enumerate(owners):
-            low = xor(me, k) * PAGES_DEV
+            low = owner(k) * PAGES_DEV
             held = jnp.where((my_ids >= low) & (my_ids < low + PAGES_DEV), 1.0, 0.0).astype(F32)
             count = jnp.sum(held, axis=1, keepdims=True)
             for cap in range(2):
@@ -231,15 +230,15 @@
 
     def load_prefix(j):
         for i, k in enumerate(CHUNK_OWNERS[j]):
-            if k in FAR:
-                passed_on(k, k + 1 - later_half).wait_recv()
-            elif k and k - 1 not in FAR:
+            if k - 1 in FAR:
+                passed_on(k - 1, slot_of(k)).wait_recv()
+            elif k and k not in FAR:
                 pool_copies[k].wait_recv()
         for i, k in enumerate(CHUNK_OWNERS[j]):
             for cap in range(2):
                 at = (2 * i + cap) * TOK
-                kaug[j, at:at + TOK, :HEAD_DIM] = kv_v[k, 0, cap]
-                load_values(j + (j > 2), 2 * i + cap, kv_v[k, 1, cap])
+                kaug[j, at:at + TOK, :HEAD_DIM] = kv_v[slot_of(k), 0, cap]
+                load_values(j + (j > 2), 2 * i + cap, kv_v[slot_of(k), 1, cap])
 
     def load_span():
         local[3].wait()
@@ -261,10 +260,9 @@
             load_values(3, k, span_v[at, 1])
 
     def scores(chunk, block, half, s_ref, x_ref):
-        if isinstance(chunk, int):
-            at = 3 if chunk == LAST else chunk
-        else:
-            at = jnp.where(chunk == SPAN, 4 + block, chunk)
+        at = chunk
+        if isinstance(chunk, int) and chunk >= SPAN:
+            at = 4 + block if chunk == SPAN else 3
         s = lax.dot_general(
             kaug[at], qaug[block, half * ROWS:(half + 1) * ROWS, :],
             (((1,), (1,)), ((), ())), preferred_element_type=F32)
@@ -313,12 +311,24 @@
     load_block(0)
     load_prefix(0)
     send_pages(1)
+    q_copies[3].start()
+
+    @pl.when(ctx < 4)
+    def _():
+        for k in (4, 5, 7, 6):
+            span_copies[k, 0].start()
+            span_copies[k, 1].start()
+
 
     def step(u, _):
-        @pl.when(u == 8)
+        for at, wave in ((1, 2), (2, 3), (4, 4)):
+            @pl.when(u == at)
+            def _():
+                send_pages(wave)
+
+        @pl.when(u == 3)
         def _():
             pass_on()
-            load_span()
 
         for at, slot in ((1, 1), (2, 2), (6, 3)):
             @pl.when(u == at)
@@ -330,42 +340,40 @@
         def _():
             load_prefix(1)
 
-        @pl.when(u == 1)
-        def _():
-            q_copies[3].start()
-
-        @pl.when(u == 2)
+        @pl.when(u == 5)
         def _():
             send_span()
-
-        @pl.when(u == 4)
-        def _():
-            send_pages(2)
 
         body(schedule(u), schedule(jnp.maximum(u - 1, 0)))
         return 0
 
-    lax.fori_loop(0, 12, step, 0)
+    lax.fori_loop(0, 8, step, 0)
 
     def finish(i, _):
         block = 3 - i
 
         @pl.when(i == 0)
         def _():
+            load_span()
+
+        before = jnp.where(i == 0, 1, 2)
+        body((SPAN, block), (before, jnp.minimum(block + 1, 3)))
+
+        @pl.when(i > 0)
+        def _():
+            send(block + 1, 1)
+
+        @pl.when(i == 0)
+        def _():
+            load_prefix(3)
+
+        body((LAST, block), (SPAN, block))
+
+        @pl.when(i == 0)
+        def _():
             load_prefix(2)
 
-        before = jnp.where(i == 0, SPAN, LAST)
-        body((2, block), (before, jnp.minimum(block + 1, 3)))
-
-        @pl.when(i > 0)
-        def _():
-            send(block + 1, 1)
-
-        @pl.when(i == 0)
-        def _():
-            load_prefix(3)
-
-        body((LAST, block), (2, block))
+        body((2, block), (LAST, block))
 
         @pl.when(i < 3)
         def _():
@@ -375,7 +383,7 @@
 
     lax.fori_loop(0, 4, finish, 0)
     keep(0)
-    absorb(LAST, 0, 1, s1, x1)
+    absorb(2, 0, 1, s1, x1)
     keep(1)
     own_copy = pltpu.make_async_copy(own_v, own_ref, loc_sem.at[5])
     own_copy.start()

time: 57 us -> 54.6 us (0.958)
  the two profiles are of different devices: /device:TPU:7 before, /device:TPU:4 now
where the time goes in v4:
time: 54.6 us; the launch traced here: 54.4 us
  Pallas kernels  54.4 us (100%)
    pallas_call x1, Pallas kernels, attend(): pl.pallas_call(kernel, out_shape=(jax.ShapeDtypeStruct((TOK, HEADS * HEAD...  51.8 us
    pallas_call x1, Pallas kernels, attend(): pl.pallas_call(convert, out_shape=jax.ShapeDtypeStruct((1, TOK, HEADS * H...  2.53 us

profile of v4, /device:TPU:4, one launch (start us, length us, event | category | flops | bytes accessed | tf_op | source)
XLA Modules:
  0.0 54.4 jit_solution(1813976770353396606)
XLA Ops:
  0.0 51.8 %attend.1 = (bf16[128,4096]{1,0:T(8,128)(2,1)}, f32[128,1024]{1,0:T(8,128)}) custom-call(s32[16,32]{1,0:T(8,128)} %ids_ref.1, s32[16]{0:T(128)} %npages.1, s32[16,32]{1,0:T(8,128)} %ids_ref.1, bf16[1,128,4096]{2,1,0:T(8,128)(2,1)} %q_ref.1, bf16[1,128,512]{2,1,0:T(8,128)(2,1)} %sk_ref.1, bf16[1,128,512]{2,1,0:T(8,128)(2,1)} %sv_ref.1, ...), custom_call_target="tpu_custom_call" | custom-call | tf_op jit(solution)/shard_map/attend/pallas_call | solution.py:419
  51.9 2.5 %convert.1 = f32[1,128,4096]{2,1,0:T(8,128)} custom-call(bf16[128,4096]{1,0:T(8,128)(2,1)} %get-tuple-element.7.far_ref, f32[128,1024]{1,0:T(8,128)} %get-tuple-element.8.own_ref), custom_call_target="tpu_custom_call" | custom-call | tf_op jit(solution)/shard_map/convert/pallas_call | solution.py:461

commit v5 on v4

--- a/solution.py
+++ b/solution.py
@@ -117,6 +117,19 @@
         return 0
 
     lax.fori_loop(0, 16, scan, 0)
+    local[0].wait()
+    local[1].wait()
+
+    def pick(k, dst):
+        r = owner(k)
+        slot = slot_of(k)
+        for cap in range(2):
+            page = pgs[r, cap]
+            dst[slot, 0, cap] = pool_v[0, page]
+            dst[slot, 1, cap] = pool_v[1, page]
+
+    for k in WAVES[0]:
+        pick(k, send_v)
     pl.semaphore_wait(barrier, sum(map(len, WAVES)) + 7)
 
     q_copies = {}
@@ -129,17 +142,6 @@
     q_copies[1].start()
     q_copies[2].start()
 
-    local[0].wait()
-    local[1].wait()
-
-    def pick(k, dst):
-        r = owner(k)
-        slot = slot_of(k)
-        for cap in range(2):
-            page = pgs[r, cap]
-            dst[slot, 0, cap] = pool_v[0, page]
-            dst[slot, 1, cap] = pool_v[1, page]
-
     pool_copies = {}
     for wave in WAVES:
         for k in wave:
@@ -164,10 +166,8 @@
         for k in WAVES[wave]:
             pool_copies[k].start()
 
-    for k in WAVES[0]:
-        pick(k, send_v)
+    send_pages(0)
     pick(0, kv_v)
-    send_pages(0)
 
     span_copies = {}
     for k in range(1, 8):
@@ -356,7 +356,7 @@
         def _():
             load_span()
 
-        before = jnp.where(i == 0, 1, 2)
+        before = jnp.where(i == 0, 1, LAST)
         body((SPAN, block), (before, jnp.minimum(block + 1, 3)))
 
         @pl.when(i > 0)
@@ -365,15 +365,15 @@
 
         @pl.when(i == 0)
         def _():
+            load_prefix(2)
+
+        body((2, block), (SPAN, block))
+
+        @pl.when(i == 0)
+        def _():
             load_prefix(3)
 
-        body((LAST, block), (SPAN, block))
-
-        @pl.when(i == 0)
-        def _():
-            load_prefix(2)
-
-        body((2, block), (LAST, block))
+        body((LAST, block), (2, block))
 
         @pl.when(i < 3)
         def _():
@@ -383,7 +383,7 @@
 
     lax.fori_loop(0, 4, finish, 0)
     keep(0)
-    absorb(2, 0, 1, s1, x1)
+    absorb(LAST, 0, 1, s1, x1)
     keep(1)
     own_copy = pltpu.make_async_copy(own_v, own_ref, loc_sem.at[5])
     own_copy.start()

time: 54.6 us -> 54.2 us (level)
  the two profiles are of different devices: /device:TPU:4 before, /device:TPU:36 now
where the time goes in v5:
time: 54.2 us; the launch traced here: 54 us
  Pallas kernels  54 us (100%)
    pallas_call x1, Pallas kernels, attend(): pl.pallas_call(kernel, out_shape=(jax.ShapeDtypeStruct((TOK, HEADS * HEAD...  51.5 us
    pallas_call x1, Pallas kernels, attend(): pl.pallas_call(convert, out_shape=jax.ShapeDtypeStruct((1, TOK, HEADS * H...  2.53 us

profile of v5, /device:TPU:36, one launch (start us, length us, event | category | flops | bytes accessed | tf_op | source)
XLA Modules:
  0.0 54.0 jit_solution(11314109507413482806)
XLA Ops:
  0.0 51.5 %attend.1 = (bf16[128,4096]{1,0:T(8,128)(2,1)}, f32[128,1024]{1,0:T(8,128)}) custom-call(s32[16,32]{1,0:T(8,128)} %ids_ref.1, s32[16]{0:T(128)} %npages.1, s32[16,32]{1,0:T(8,128)} %ids_ref.1, bf16[1,128,4096]{2,1,0:T(8,128)(2,1)} %q_ref.1, bf16[1,128,512]{2,1,0:T(8,128)(2,1)} %sk_ref.1, bf16[1,128,512]{2,1,0:T(8,128)(2,1)} %sv_ref.1, ...), custom_call_target="tpu_custom_call" | custom-call | tf_op jit(solution)/shard_map/attend/pallas_call | solution.py:419
  51.5 2.5 %convert.1 = f32[1,128,4096]{2,1,0:T(8,128)} custom-call(bf16[128,4096]{1,0:T(8,128)(2,1)} %get-tuple-element.7.far_ref, f32[128,1024]{1,0:T(8,128)} %get-tuple-element.8.own_ref), custom_call_target="tpu_custom_call" | custom-call | tf_op jit(solution)/shard_map/convert/pallas_call | solution.py:461
